TPU v7x, 256 devices: a whole 4x4x8 slice. The times are simulated.
256 devices in a mesh: rows: 64 (over z, y, core), rep: 4 (over x).
Axes of the slice: x: 4, y: 4, z: 8, core: 2. Of those that a mesh axis runs over, the one named last changes fastest.
Arguments:
- features: bfloat16 [262144, 256], P(('rows', 'rep')), may hold values from -6 to 6
- weight: bfloat16 [256, 256], replicated, may hold values from -0.375 to 0.375
- block_cols: int32 [2048, 4, 2], P('rows', 'rep'), may hold values from 0 to 511, as said below
- block_vals: bfloat16 [2048, 4, 2, 128, 128], P('rows', 'rep'), as said below
- out_grad: bfloat16 [262144, 256], P('rows'), may hold values from -6 to 6
Outputs:
- activations: bfloat16 [262144, 256], P(('rows', 'rep'))
- input_grad: bfloat16 [262144, 256], P(('rows', 'rep'))
- weight_grad: float32 [256, 256], replicated
Inputs may be any that keep to these rules, and one draw needn't show every extreme that they name: `block_cols`: layer c's k-th block column is global block column (k // 8) * 32 + c * 8 + k % 8, whose rows the device of index k // 8 along rows holds in layer c. In the layer that owns a block row, slot 0 is its diagonal block; no other held block of a device lies in its own block columns. For every layer, every device along rows and every other device along rows, at most 1 of the first device's held blocks in that layer lie in block columns of the other, and in every draw some pair has exactly 1. `block_vals`: the adjacency is symmetric: every held block at block row b, block column g in slot s has a partner held at block row g, block column b in slot s (of the layer owning b) that is its transpose; diagonal blocks are symmetric.
All inputs are finite; a program needn't handle non-finite values.
Results may differ from a plain program's by a relative error of at most 0.006.
Values may be sent and summed in bfloat16 or wider, within the bound.
A program may use at most 128 MiB of HBM per device.

v0:
```python
import math

import jax
import jax.numpy as jnp
from jax import lax
from jax.sharding import PartitionSpec as P


def silu_parts(summed):
    sigmoid_vals = jax.nn.sigmoid(summed)
    return (summed * sigmoid_vals, sigmoid_vals * (1.0 + summed * (1.0 - sigmoid_vals)))


def apply_blocks(local_vals, fetched):
    product = jnp.einsum("bsij,bsjf->bif", local_vals, fetched, preferred_element_type=jnp.float32)
    return product.reshape(-1, fetched.shape[-1])


def serve_blocks(source_rows, asked_places, block_size):
    feature_width = source_rows.shape[1]
    blocks = source_rows.reshape(-1, block_size, feature_width)
    flat_ask = asked_places.reshape(-1)
    picked = jnp.take(blocks, jnp.clip(flat_ask, 0, blocks.shape[0] - 1), axis=0)
    picked = jnp.where((flat_ask >= 0)[:, None, None], picked, jnp.zeros_like(picked))
    return picked


def on_device(features, weight, block_cols, block_vals, out_grad):
    own_rows, feature_width = features.shape
    block_size = block_vals.shape[-1]
    row_blocks, slot_count = (block_cols.shape[0], block_cols.shape[2])
    own_blocks = own_rows // block_size
    peer_count = lax.axis_size("rows")
    layer_count = lax.axis_size("rep")
    couple_total = ((layer_count - 1) * slot_count * own_blocks + own_blocks) // 2
    reach_classes = peer_count // 2 - 1
    capacity = (couple_total + reach_classes - 1) // reach_classes
    my_group = lax.axis_index("rows")
    layer_index = lax.axis_index("rep")
    local_vals = block_vals[:, 0]
    flat_cols = block_cols[:, 0].reshape(-1)
    request_total = flat_cols.shape[0]
    owners = flat_cols // own_blocks
    places = flat_cols % own_blocks
    remote = owners != my_group
    positions = jnp.arange(request_total, dtype=jnp.int32)
    same_owner = (owners[:, None] == owners[None, :]) & (positions[:, None] > positions[None, :])
    owner_ranks = jnp.sum(same_owner.astype(jnp.int32), axis=1)
    slot_keys = jnp.where(remote, owners * capacity + owner_ranks, -1)
    slot_table = jnp.arange(peer_count * capacity, dtype=jnp.int32)
    matches = slot_keys[:, None] == slot_table[None, :]
    requests = (jnp.sum(jnp.where(matches, places[:, None] + 1, 0), axis=0) - 1).reshape(
        peer_count, capacity
    )
    asked_places = lax.all_to_all(requests, "rows", split_axis=0, concat_axis=0, tiled=True)
    mixed_rows = jnp.dot(features, weight, preferred_element_type=jnp.float32).astype(jnp.bfloat16)
    arrived = lax.all_to_all(
        serve_blocks(mixed_rows, asked_places, block_size),
        "rows",
        split_axis=0,
        concat_axis=0,
        tiled=True,
    )
    from_peers = jnp.take(arrived, jnp.clip(slot_keys, 0, arrived.shape[0] - 1), axis=0)
    from_self = jnp.take(mixed_rows.reshape(own_blocks, block_size, feature_width), places, axis=0)
    joined = jnp.where(remote[:, None, None], from_peers, from_self)
    partial_sum = apply_blocks(
        local_vals, joined.reshape(row_blocks, slot_count, block_size, feature_width)
    )
    share_start = layer_index * own_rows
    summed = lax.psum(partial_sum, "rep")
    values_all, slopes_all = silu_parts(summed)
    grad_rows = (out_grad.astype(jnp.float32) * slopes_all).astype(jnp.bfloat16)
    activated = lax.dynamic_slice_in_dim(values_all, share_start, own_rows, 0).astype(jnp.bfloat16)
    slot_terms = jnp.einsum(
        "bsji,bjf->bsif",
        local_vals,
        grad_rows.reshape(row_blocks, block_size, feature_width),
        preferred_element_type=jnp.float32,
    ).reshape(request_total, block_size, feature_width)
    filler = jnp.sum(jnp.where(matches, positions[:, None], 0), axis=0)
    filled = jnp.any(matches, axis=0)
    outgoing = jnp.where(
        filled[:, None, None], jnp.take(slot_terms, filler, axis=0), jnp.zeros((), jnp.float32)
    )
    returned = lax.all_to_all(outgoing, "rows", split_axis=0, concat_axis=0, tiled=True)
    block_span = block_size * feature_width
    own_index = jnp.arange(own_blocks, dtype=jnp.int32)
    arrive_hot = (asked_places.reshape(-1)[:, None] == own_index[None, :]).astype(jnp.float32)
    self_hot = ((~remote)[:, None] & (places[:, None] == own_index[None, :])).astype(jnp.float32)
    collected = jnp.einsum(
        "qo,qx->ox", arrive_hot, returned.reshape(-1, block_span), precision=lax.Precision.HIGHEST
    )
    self_terms = jnp.einsum(
        "no,nx->ox", self_hot, slot_terms.reshape(-1, block_span), precision=lax.Precision.HIGHEST
    )
    back_rows = (collected + self_terms).reshape(own_rows, feature_width)
    node_total = own_rows * peer_count * layer_count
    local_weight = jnp.dot(
        features.astype(jnp.float32).T, back_rows, precision=lax.Precision.HIGHEST
    )
    weight_grad = lax.psum(local_weight, ("rows", "rep")) * (1.0 / math.sqrt(node_total))
    input_grad = jnp.dot(
        back_rows.astype(jnp.bfloat16), weight.T, preferred_element_type=jnp.float32
    ).astype(jnp.bfloat16)
    return (activated, input_grad, weight_grad)


def solution(mesh):
    placed = (
        P(("rows", "rep"), None),
        P(),
        P("rows", "rep", None),
        P("rows", "rep", None, None, None),
        P("rows", None),
    )
    return jax.shard_map(
        on_device,
        mesh=mesh,
        in_specs=placed,
        out_specs=(P(("rows", "rep"), None), P(("rows", "rep"), None), P()),
        check_vma=False,
    )
```

profile of v0, /device:TPU:1, one launch (start us, length us, event | category | flops | bytes accessed | tf_op | source)
XLA Modules:
  0.0 754.5 jit_solution(3216159301547902736)
XLA Ops:
  7.2 0.9 copy.37
  9.3 13.2 %all-to-all-start = ((s32[64,1,1]{2,1,0:T(1,128)}), s32[64,1,1]{2,1,0:T(1,128)S(1)}, u32[]{:S(2)}, u32[]{:S(2)}) async-start(s32[64,1,1]{2,1,0:T(1,128)} %copy.38), calls=%async_computation | async-start | bytes 65536 | tf_op jit(solution)/shard_map/all_to_all | solution.py:55
  22.4 1.3 convolution_convert_fusion.1
  23.8 7.9 %all-to-all-done = s32[64,1,1]{2,1,0:T(1,128)S(1)} async-done(((s32[64,1,1]{2,1,0:T(1,128)}), s32[64,1,1]{2,1,0:T(1,128)S(1)}, u32[]{:S(2)}, u32[]{:S(2)}) %all-to-all-start) | async-done | bytes 288 | tf_op jit(solution)/shard_map/all_to_all | solution.py:55
  31.7 1.2 reduce.1
  33.0 2.8 gather_fusion.2
  35.7 1.2 compare_reduce_fusion
  37.0 4.0 select_select_fusion.2
  40.9 5.7 all-to-all-start.1
  47.0 2.8 gather_fusion.3
  49.8 91.5 %all-to-all-done.1 = bf16[64,128,256]{2,1,0:T(8,128)(2,1)} async-done(((bf16[64,128,256]{2,1,0:T(8,128)(2,1)}), bf16[64,128,256]{2,1,0:T(8,128)(2,1)}, u32[]{:S(2)}, u32[]{:S(2)}) %all-to-all-start.1) | async-done | bytes 4194336 | tf_op jit(solution)/shard_map/all_to_all | solution.py:57
  141.3 5.0 gather_fusion
  146.3 4.1 select_select_fusion.1
  150.3 2.8 fusion.2
  153.3 95.6 %all-reduce.3.cloned.1.call-done = f32[4096,256]{1,0:T(8,128)} async-done(((f32[4096,256]{1,0:T(8,128)}), f32[4096,256]{1,0:T(8,128)}) %all-reduce.3.cloned.1.call-update) | async-done | bytes 4194320 | tf_op jit(solution)/shard_map/psum | solution.py:71
  248.9 6.4 multiply_convert_fusion
  255.3 4.5 fusion
  259.8 9.0 %copy.41 = f32[64,128,256]{2,1,0:T(8,128)} copy(f32[64,128,256]{1,2,0:T(8,128)} %bitcast.59) | data formatting | bytes 16777216 | tf_op jit(solution)/shard_map/reshape | solution.py:80
  268.8 7.7 %gather_fusion.1 = f32[64,128,256]{2,1,0:T(8,128)} fusion(f32[64,128,256]{2,1,0:T(8,128)} %copy.41, s32[1024]{0:T(1024)S(1)} %pad_clamp_fusion), kind=kCustom, calls=%fused_computation.3 | custom fusion | bytes 16777472 | tf_op jit(solution)/shard_map/jit(_take)/gather | solution.py:84
  276.5 8.5 %select_select_fusion = f32[64,128,256]{2,1,0:T(8,128)} fusion(f32[64,128,256]{2,1,0:T(8,128)} %gather_fusion.1, pred[64]{0:T(512)(128)(4,1)S(1)} %compare_and_fusion.2, pred[64]{0:T(512)(128)(4,1)S(1)} %fusion.6), kind=kLoop, calls=%fused_computation.5 | loop fusion | flops 4194304 | bytes 16777344 | tf_op jit(solution)/shard_map/jit(_where)/select_n | solution.py:83
  285.0 10.9 %all-to-all-start.2 = ((f32[64,128,256]{2,1,0:T(8,128)}), f32[64,128,256]{2,1,0:T(8,128)}, u32[]{:S(2)}, u32[]{:S(2)}) async-start(f32[64,128,256]{2,1,0:T(8,128)} %select_select_fusion), calls=%async_computation.2 | async-start | bytes 16777216 | tf_op jit(solution)/shard_map/all_to_all | solution.py:86
  295.9 9.2 %copy.49 = f32[8,8,128,256]{3,1,2,0:T(8,128)} copy(f32[8,8,128,256]{2,3,1,0:T(8,128)} %bitcast.60) | data formatting | bytes 16777216
  305.1 2.4 fusion.4
  307.6 170.7 %all-to-all-done.2 = f32[64,128,256]{2,1,0:T(8,128)} async-done(((f32[64,128,256]{2,1,0:T(8,128)}), f32[64,128,256]{2,1,0:T(8,128)}, u32[]{:S(2)}, u32[]{:S(2)}) %all-to-all-start.2) | async-done | bytes 8388640 | tf_op jit(solution)/shard_map/all_to_all | solution.py:86
  478.3 8.3 %copy.48 = f32[8,8,128,256]{3,1,2,0:T(8,128)S(1)} copy(f32[8,8,128,256]{3,2,1,0:T(8,128)} %bitcast.25) | data formatting | bytes 16777216
  486.5 2.9 fusion.8
  489.5 3.9 convolution_add_fusion
  493.3 1.4 reshape.298
  494.8 2.7 convolution_bitcast_fusion
  497.5 1.1 convolution_convert_fusion
  498.7 247.2 %all-reduce.5.cloned.1.call-done = f32[256,256]{0,1:T(8,128)} async-done(((f32[256,256]{0,1:T(8,128)}), f32[256,256]{0,1:T(8,128)}) %all-reduce.5.cloned.1.call-update) | async-done | bytes 262160 | tf_op jit(solution)/shard_map/psum | solution.py:102
  745.9 1.0 broadcast_multiply_fusion
  (34 shorter events, 2.6 us)
Async XLA Ops:
  7.2 143.2 %copy-start = (bf16[32,1,2,128,128]{4,3,2,1,0:T(8,128)(2,1)S(1)}, bf16[32,1,2,128,128]{4,3,2,1,0:T(8,128)(2,1)}, u32[]{:S(2)}) copy-start(bf16[32,1,2,128,128]{4,3,2,1,0:T(8,128)(2,1)} %param.10) | copy-start | bytes 6291460
  9.3 22.5 %all-to-all-start = ((s32[64,1,1]{2,1,0:T(1,128)}), s32[64,1,1]{2,1,0:T(1,128)S(1)}, u32[]{:S(2)}, u32[]{:S(2)}) async-start(s32[64,1,1]{2,1,0:T(1,128)} %copy.38), calls=%async_computation | async-start | bytes 65536 | tf_op jit(solution)/shard_map/all_to_all | solution.py:55
  40.9 100.4 %all-to-all-start.1 = ((bf16[64,128,256]{2,1,0:T(8,128)(2,1)}), bf16[64,128,256]{2,1,0:T(8,128)(2,1)}, u32[]{:S(2)}, u32[]{:S(2)}) async-start(bf16[64,128,256]{2,1,0:T(8,128)(2,1)} %select_select_fusion.2), calls=%async_computation.1 | async-start | bytes 8388608 | tf_op jit(solution)/shard_map/all_to_all | solution.py:57
  46.6 202.2 %all-reduce.3.cloned.1.call-start = ((), (), s32[]{:S(2)}) async-start(), calls=%async_computation.3 | async-start | bytes 8388608 | tf_op jit(solution)/shard_map/psum | solution.py:71
  285.0 193.3 %all-to-all-start.2 = ((f32[64,128,256]{2,1,0:T(8,128)}), f32[64,128,256]{2,1,0:T(8,128)}, u32[]{:S(2)}, u32[]{:S(2)}) async-start(f32[64,128,256]{2,1,0:T(8,128)} %select_select_fusion), calls=%async_computation.2 | async-start | bytes 16777216 | tf_op jit(solution)/shard_map/all_to_all | solution.py:86
  295.9 450.0 %all-reduce.5.cloned.1.call-start = ((), (), s32[]{:S(2)}) async-start(), calls=%async_computation.4 | async-start | bytes 524288 | tf_op jit(solution)/shard_map/psum | solution.py:102
  478.3 11.2 %slice-start = ((s8[8388608]{0:T(1024)(128)(4,1)}), s8[4194304]{0:T(1024)(128)(4,1)S(1)}, s32[]{:S(2)}) async-start(s8[8388608]{0:T(1024)(128)(4,1)} %bitcast.63), calls=%async_computation.5 | async-start | bytes 8388608
  478.3 11.2 %slice-start.1 = ((s8[8388608]{0:T(1024)(128)(4,1)}), s8[4194304]{0:T(1024)(128)(4,1)S(1)}, s32[]{:S(2)}) async-start(s8[8388608]{0:T(1024)(128)(4,1)} %bitcast.63), calls=%async_computation.6 | async-start | bytes 8388608
  489.5 258.2 %copy-start.1 = (bf16[32,1,2,128,128]{4,3,2,1,0:T(8,128)(2,1)S(1)}, bf16[32,1,2,128,128]{4,3,2,1,0:T(8,128)(2,1)}, u32[]{:S(2)}) copy-start(bf16[32,1,2,128,128]{4,3,2,1,0:T(8,128)(2,1)} %param.10) | copy-start | bytes 6291460
  493.3 4.2 copy-start.2
Sparse Core Ops, SparseCore 0:
  153.3 95.5 all-reduce.2
  497.7 248.1 all-reduce.4
where the time goes:
time: 756 us; the launch traced here: 755 us
  waiting for transfers between devices  613 us (81%)
  local copies, waits for them, and re-layouts  48.7 us (6%)
  starting transfers between devices  30 us (4%)
  other arithmetic  29.3 us (4%)
  matrix products  19.3 us (3%)
  between operations  14.2 us (2%)
    psum x1, waiting for transfers between devices, on_device(): lax.psum(local_weight, ('rows', 'rep')) * (1.0 / math.sqrt(node_total))  247 us
    all_to_all x1, waiting for transfers between devices, on_device(): lax.all_to_all(outgoing, 'rows', split_axis=0, concat_axis=0, tiled=True)  171 us
    psum x1, waiting for transfers between devices, on_device(): summed = lax.psum(partial_sum, 'rep')  95.6 us
    all_to_all x1, waiting for transfers between devices, on_device(): lax.all_to_all(serve_blocks(mixed_rows, asked_places, block_size), 'rows'...  91.5 us
    unnamed x14, local copies, waits for them, and re-layouts  19.2 us
  transfers between devices with their start and end apart: 5, of which 5 were waited for; matrix products, arithmetic and copies ran while one was open for 2% of the time, Pallas kernels for 0%

commit v1 on v0

v1 whole, which is shorter than its diff:
```python
import functools
import math

import jax
import jax.numpy as jnp
from jax import lax
from jax.experimental import pallas as pl
from jax.experimental.pallas import tpu as pltpu
from jax.sharding import PartitionSpec as P

MESH = pl.DeviceIdType.MESH
Z = 8
YC = 8
X = 4
B = 128
LANES = 128
OWN = 8
F32 = jnp.float32
BF16 = jnp.bfloat16


def place():
    r, c = lax.axis_index("rows"), lax.axis_index("rep")
    return r, r // YC, r % YC, c


def greet(partners):
    barrier = pltpu.get_barrier_semaphore()
    for device in partners:
        pl.semaphore_signal(barrier, inc=1, device_id=device, device_id_type=MESH)
    pl.semaphore_wait(barrier, len(partners))


def remote(src, dst, send, recv, device):
    return pltpu.make_async_remote_copy(
        src_ref=src, dst_ref=dst, send_sem=send, recv_sem=recv, device_id=device, device_id_type=MESH
    )


def wait_bytes(ref, sem):
    pltpu.make_async_copy(ref, ref, sem).wait()


def table_kernel(own_ref, out_ref, got, send, recv):
    r, z, yc, c = place()
    greet([(z * YC + (yc + 1 + j) % YC, c) for j in range(YC - 1)])
    copies = [
        remote(own_ref, got.at[j], send.at[j], recv.at[j], (z * YC + (yc + 1 + j) % YC, c)) for j in range(YC - 1)
    ]
    for copy in copies:
        copy.start()
    for copy in copies:
        copy.wait()
    out_ref[0 : YC - 1] = got[...]
    out_ref[YC - 1] = own_ref[...]


def exchange_tables(own):
    return pl.pallas_call(
        table_kernel,
        out_shape=jax.ShapeDtypeStruct((YC, 8, LANES), jnp.int32),
        in_specs=[pl.BlockSpec(memory_space=pltpu.VMEM)],
        out_specs=pl.BlockSpec(memory_space=pltpu.VMEM),
        scratch_shapes=[
            pltpu.VMEM((YC - 1, 8, LANES), jnp.int32),
            pltpu.SemaphoreType.DMA((YC - 1,)),
            pltpu.SemaphoreType.DMA((YC - 1,)),
        ],
        compiler_params=pltpu.CompilerParams(collective_id=0, has_side_effects=True),
    )(own)


def spmm_kernel(tab, idx, x_ref, vals_ref, out_ref, *scratch):
    ag = [scratch[h * Z : (h + 1) * Z] for h in range(2)]
    sbuf, src, xs, xr, own = (scratch[16 + 2 * i : 18 + 2 * i] for i in range(5))
    z_send, z_recv, y_send, y_recv, x_send, x_recv = scratch[26:]
    r, z, yc, c = place()
    up, down = (z + 1) % Z * YC + yc, (z + Z - 1) % Z * YC + yc
    greet(
        [(up, c), (down, c)]
        + [(z * YC + (yc + 1 + j) % YC, c) for j in range(YC - 1)]
        + [(r, (c + d) % X) for d in range(1, X)]
    )
    half = OWN // 2

    def hop(h, k, forward):
        source = x_ref.at[:, :, pl.ds(h * LANES, LANES)] if k == 0 else ag[h][k]
        nxt = (k + 1) % Z if forward else (k - 1) % Z
        target = ag[h][nxt]
        lane = 0 if forward else 1
        if nxt == Z // 2:
            rows = pl.ds(0, half) if forward else pl.ds(half, half)
            source, target = source.at[rows], target.at[rows]
        return remote(
            source, target, z_send.at[h, nxt, lane], z_recv.at[h, nxt, lane], (up if forward else down, c)
        )

    def arrived(h, k, lane):
        if k == Z // 2:
            part = ag[h][k].at[pl.ds(0 if lane == 0 else half, half)]
        else:
            part = ag[h][k]
        wait_bytes(part, z_recv.at[h, k, lane])

    def load_block(h, k, p):
        if k == 0:
            return x_ref[p, :, pl.ds(h * LANES, LANES)]
        return ag[h][k][p]

    def serve(h, k):
        column = (z - k + Z) % Z * YC + yc

        def pick(j, _):
            sbuf[h][j * Z + k] = load_block(h, k, tab[YC - 2 - j, column])
            return 0

        lax.fori_loop(0, YC - 1, pick, 0)
        if k == 0:
            for p in range(OWN):
                src[h][YC * Z + p] = x_ref[p, :, pl.ds(h * LANES, LANES)]
        else:
            src[h][(YC - 1) * Z + k] = load_block(h, k, tab[YC - 1, column])

        def post(j, _):
            remote(
                sbuf[h].at[j * Z + k],
                src[h].at[j * Z + k],
                y_send.at[h],
                y_recv.at[h],
                (z * YC + (yc + 1 + j) % YC, c),
            ).start()
            return 0

        lax.fori_loop(0, YC - 1, post, 0)

    def products(h, d):
        first = (c + d) % X * OWN

        def row(p, _):
            b = first + p
            total = jnp.dot(vals_ref[b, 0], src[h][idx[2 * b]], preferred_element_type=F32)
            total += jnp.dot(vals_ref[b, 1], src[h][idx[2 * b + 1]], preferred_element_type=F32)
            if d == 0:
                own[h][p] = total
            else:
                xs[h][(d - 1) * OWN + p] = total
                slot = (d - 1) * OWN + p
                remote(
                    xs[h].at[slot], xr[h].at[slot], x_send.at[h], x_recv.at[h], (r, (c + d) % X)
                ).start()
            return 0

        lax.fori_loop(0, OWN, row, 0)

    def collect(h):
        wait_bytes(xr[h], x_recv.at[h])

        def row(p, _):
            out_ref[p, :, pl.ds(h * LANES, LANES)] = (own[h][p] + xr[h][p]) + (xr[h][OWN + p] + xr[h][2 * OWN + p])
            return 0

        lax.fori_loop(0, OWN, row, 0)

    def ring(h, step):
        if step < Z // 2:
            arrived(h, step, 0)
            hop(h, step, True).start()
            arrived(h, Z - step, 1)
            hop(h, Z - step, False).start()
            serve(h, step)
            serve(h, Z - step)
        else:
            arrived(h, step, 0)
            arrived(h, step, 1)
            serve(h, step)

    def begin(h):
        hop(h, 0, True).start()
        hop(h, 0, False).start()

    begin(0)
    serve(0, 0)
    ring(0, 1)
    begin(1)
    serve(1, 0)
    ring(0, 2)
    ring(1, 1)
    ring(0, 3)
    ring(1, 2)
    ring(0, 4)
    wait_bytes(src[0].at[pl.ds(0, (YC - 1) * Z)], y_recv.at[0])
    products(0, 2)
    ring(1, 3)
    products(0, 1)
    products(0, 3)
    products(0, 0)
    ring(1, 4)
    wait_bytes(src[1].at[pl.ds(0, (YC - 1) * Z)], y_recv.at[1])
    for d in (2, 1, 3, 0):
        products(1, d)
    collect(0)
    collect(1)
    for h in range(2):
        for k in range(Z // 2):
            hop(h, k, True).wait_send()
            hop(h, (Z - k) % Z, False).wait_send()
        wait_bytes(sbuf[h], y_send.at[h])
        wait_bytes(xs[h], x_send.at[h])


def spmm(tab, idx, x, vals):
    blocks = lambda n, kind: pltpu.VMEM((n, B, LANES), kind)
    smem = pl.BlockSpec(memory_space=pltpu.SMEM)
    vmem = pl.BlockSpec(memory_space=pltpu.VMEM)
    return pl.pallas_call(
        spmm_kernel,
        out_shape=jax.ShapeDtypeStruct((OWN, B, 2 * LANES), F32),
        in_specs=[smem, smem, vmem, vmem],
        out_specs=vmem,
        scratch_shapes=[blocks(OWN, BF16) for _ in range(2 * Z)]
        + [blocks((YC - 1) * Z, BF16)] * 2
        + [blocks(YC * Z + OWN, BF16)] * 2
        + [blocks((X - 1) * OWN, F32)] * 2
        + [blocks((X - 1) * OWN, F32)] * 2
        + [blocks(OWN, F32)] * 2
        + [
            pltpu.SemaphoreType.DMA((2, Z, 2)),
            pltpu.SemaphoreType.DMA((2, Z, 2)),
            pltpu.SemaphoreType.DMA((2,)),
            pltpu.SemaphoreType.DMA((2,)),
            pltpu.SemaphoreType.DMA((2,)),
            pltpu.SemaphoreType.DMA((2,)),
        ],
        compiler_params=pltpu.CompilerParams(
            collective_id=1, has_side_effects=True, vmem_limit_bytes=56 * 1024 * 1024
        ),
    )(tab, idx, x, vals)


def final_kernel(scale, f_ref, back_ref, w_ref, grad_ref, wg_ref, part, r1, a1, r2, a2, r3, r4, r5, *sems):
    s1, v1, s2, v2, s3, v3, s4, v4, s5, v5 = sems
    r, z, yc, c = place()
    peers_x = [(r, (c + d) % X) for d in range(1, X)]
    peers_y = [(z * YC + (yc + 1 + j) % YC, c) for j in range(YC - 1)]
    peers_z = [((z + 1 + i) % Z * YC + yc, c) for i in range(Z - 1)]
    greet(peers_x + peers_y + peers_z)
    width = w_ref.shape[0]
    share = width // X
    small = share // YC
    back = back_ref[...]
    high = back.astype(BF16)
    low = (back - high.astype(F32)).astype(BF16)
    contract = (((0,), (0,)), ((), ()))
    part[...] = lax.dot_general(f_ref[...], high, contract, preferred_element_type=F32) + lax.dot_general(
        f_ref[...], low, contract, preferred_element_type=F32
    )

    def share_of(d):
        return pl.ds(pl.multiple_of((c + d) % X * share, share), share)

    one = [remote(part.at[share_of(d)], r1.at[d - 1], s1.at[d - 1], v1.at[d - 1], peers_x[d - 1]) for d in range(1, X)]
    for copy in one:
        copy.start()
    grad_ref[...] = lax.dot_general(high, w_ref[...], (((1,), (1,)), ((), ())), preferred_element_type=F32).astype(BF16)
    for copy in one:
        copy.wait()
    a1[...] = (part[share_of(0)] + r1[0]) + (r1[1] + r1[2])

    def small_of(j):
        return pl.ds(pl.multiple_of((yc + 1 + j) % YC * small, small), small)

    two = [remote(a1.at[small_of(j)], r2.at[j], s2.at[j], v2.at[j], peers_y[j]) for j in range(YC - 1)]
    for copy in two:
        copy.start()
    for copy in two:
        copy.wait()
    total = a1[small_of(YC - 1)]
    for j in range(YC - 1):
        total = total + r2[j]
    a2[...] = total
    r3[z] = total
    three = [remote(a2, r3.at[z], s3.at[i], v3.at[i], peers_z[i]) for i in range(Z - 1)]
    for copy in three:
        copy.start()
    for i in range(Z - 1):
        remote(a2, r3.at[(z + Z - 1 - i) % Z], s3.at[i], v3.at[i], peers_z[i]).wait()
    total = r3[0]
    for i in range(1, Z):
        total = total + r3[i]
    r4[yc] = total * scale
    four = [remote(r4.at[yc], r4.at[yc], s4.at[j], v4.at[j], peers_y[j]) for j in range(YC - 1)]
    for copy in four:
        copy.start()
    for j in range(YC - 1):
        remote(r4.at[yc], r4.at[(yc + YC - 1 - j) % YC], s4.at[j], v4.at[j], peers_y[j]).wait()
    five = [remote(r4, r5.at[c], s5.at[d], v5.at[d], peers_x[d]) for d in range(X - 1)]
    for copy in five:
        copy.start()
    r5[c] = r4[...]
    for d in range(X - 1):
        remote(r4, r5.at[(c + X - 1 - d) % X], s5.at[d], v5.at[d], peers_x[d]).wait()
    wg_ref[...] = r5[...].reshape(width, width)


def finish(features, back, weight, node_total):
    rows, width = features.shape
    share = width // X
    small = share // YC
    vmem = pl.BlockSpec(memory_space=pltpu.VMEM)
    dma = lambda n: pltpu.SemaphoreType.DMA((n,))
    return pl.pallas_call(
        functools.partial(final_kernel, 1.0 / math.sqrt(node_total)),
        out_shape=(jax.ShapeDtypeStruct((rows, width), BF16), jax.ShapeDtypeStruct((width, width), F32)),
        in_specs=[vmem] * 3,
        out_specs=(vmem, vmem),
        scratch_shapes=[
            pltpu.VMEM((width, width), F32),
            pltpu.VMEM((X - 1, share, width), F32),
            pltpu.VMEM((share, width), F32),
            pltpu.VMEM((YC - 1, small, width), F32),
            pltpu.VMEM((small, width), F32),
            pltpu.VMEM((Z, small, width), F32),
            pltpu.VMEM((YC, small, width), F32),
            pltpu.VMEM((X, YC, small, width), F32),
        ]
        + [dma(X - 1)] * 2
        + [dma(YC - 1)] * 2
        + [dma(Z - 1)] * 2
        + [dma(YC - 1)] * 2
        + [dma(X - 1)] * 2,
        compiler_params=pltpu.CompilerParams(collective_id=2, has_side_effects=True),
    )(features, back, weight)


def silu_parts(summed):
    sigmoid_vals = jax.nn.sigmoid(summed)
    return (summed * sigmoid_vals, sigmoid_vals * (1.0 + summed * (1.0 - sigmoid_vals)))


def on_device(features, weight, block_cols, block_vals, out_grad):
    own_rows, width = features.shape
    r, z, yc, c = place()
    flat = block_cols[:, 0].reshape(-1)
    owners, places = flat // OWN, flat % OWN
    slot = (yc + YC - 1 - owners % YC) % YC * Z + (z + Z - owners // YC) % Z
    idx = jnp.where(owners == r, YC * Z + places, slot)
    groups = jnp.arange(LANES, dtype=jnp.int32)
    wanted = (owners[:, None] == groups[None, :]) & (owners != r)[:, None]
    table = jnp.sum(jnp.where(wanted, places[:, None], 0), axis=0)
    tab = exchange_tables(jnp.broadcast_to(table[None], (8, LANES)))[:, 0]
    vals = block_vals[:, 0]
    mixed = jnp.dot(features, weight, preferred_element_type=F32).astype(BF16)
    summed = spmm(tab, idx, mixed.reshape(OWN, B, width), vals).reshape(own_rows, width)
    values, slopes = silu_parts(summed)
    own_grad = lax.dynamic_slice_in_dim(out_grad, c * own_rows, own_rows, 0)
    masked = (own_grad.astype(F32) * slopes).astype(BF16)
    back = spmm(tab, idx, masked.reshape(OWN, B, width), vals).reshape(own_rows, width)
    input_grad, weight_grad = finish(features, back, weight, own_rows * Z * YC * X)
    return (values.astype(BF16), input_grad, weight_grad)


def solution(mesh):
    placed = (
        P(("rows", "rep"), None),
        P(),
        P("rows", "rep", None),
        P("rows", "rep", None, None, None),
        P("rows", None),
    )
    return jax.shard_map(
        on_device,
        mesh=mesh,
        in_specs=placed,
        out_specs=(P(("rows", "rep"), None), P(("rows", "rep"), None), P()),
        check_vma=False,
    )
```

time: 756 us -> 250 us (0.33)
  waiting for transfers between devices: 613 us -> 0 us
  Pallas kernels: 0 us -> 237 us
  local copies, waits for them, and re-layouts: 48.7 us -> 6.36 us
  starting transfers between devices: 30 us -> 0 us
  other arithmetic: 29.3 us -> 3.44 us
  matrix products: 19.3 us -> 2.15 us
  between operations: 14.2 us -> 0.69 us
    psum x2 -> x0, waiting for transfers between devices: 343 us -> none  [the longest x1 247 us: on_device(): lax.psum(local_weight, ('rows', 'rep')) * (1.0 / math.sqrt(node_total))]
    all_to_all x3 -> x0, waiting for transfers between devices: 270 us -> none  [the longest x1 171 us: on_device(): lax.all_to_all(outgoing, 'rows', split_axis=0, concat_axis=0, tiled=True)]
    pallas_call x0 -> x4, Pallas kernels: none -> 237 us  [the longest x2 199 us: spmm(): pl.pallas_call(spmm_kernel, out_shape=jax.ShapeDtypeStruct((OWN, B, 2 * L...]
    all_to_all x3 -> x0, starting transfers between devices: 29.7 us -> none  [the longest x1 13.2 us: on_device(): lax.all_to_all(requests, 'rows', split_axis=0, concat_axis=0, tiled=True)]
    gather x4 -> x0, local copies, waits for them, and re-layouts: 18.2 us -> none  [the longest x1 7.67 us: on_device(): jnp.take(slot_terms, filler, axis=0)]
    dot_general x7 -> x1, matrix products: 19.3 us -> 2.15 us  [on_device(): mixed = jnp.dot(features, weight, preferred_element_type=F32).astype(BF16)]
    select_n x5 -> x1, other arithmetic: 16.6 us -> 0.55 us  [on_device(): idx = jnp.where(owners == r, YC * Z + places, slot)]
    unnamed x14 -> x3, local copies, waits for them, and re-layouts: 19.2 us -> 4.3 us
  transfers between devices with their start and end apart: 5 -> 0, of which waited for: 5 -> 0; matrix products, arithmetic and copies ran while one was open for 2% -> 0% of each run, Pallas kernels for 0% -> 0%
where the time goes in v1:
time: 250 us
  Pallas kernels  237 us (95%)
  local copies, waits for them, and re-layouts  6.36 us (3%)
  other arithmetic  3.44 us (1%)
    pallas_call x2, Pallas kernels, spmm(): pl.pallas_call(spmm_kernel, out_shape=jax.ShapeDtypeStruct((OWN, B, 2 * L...  199 us
    pallas_call x1, Pallas kernels, finish(): pl.pallas_call(functools.partial(final_kernel, 1.0 / math.sqrt(node_total...  28.8 us
    pallas_call x1, Pallas kernels, exchange_tables(): pl.pallas_call(table_kernel, out_shape=jax.ShapeDtypeStruct((YC, 8, LANES...  9.48 us

profile of v1, /device:TPU:1, one launch (start us, length us, event | category | flops | bytes accessed | tf_op | source)
XLA Modules:
  0.0 249.6 jit_solution(13537412479750316099)
XLA Ops:
  0.7 0.8 copy.12
  1.4 0.1 reshape_squeeze.3
  1.5 0.5 compare_select_fusion.4
  2.1 0.1 select_reduce_fusion
  2.2 0.6 broadcast_in_dim.24.own_ref
  2.8 9.5 %shard_map.76 = s32[8,8,128]{2,1,0:T(8,128)} custom-call(s32[8,128]{1,0:T(8,128)} %broadcast_in_dim.24.own_ref), custom_call_target="tpu_custom_call" | custom-call | tf_op jit(solution)/shard_map/pallas_call | solution.py:59
  12.3 1.4 slice.3
  13.6 2.2 convolution_convert_fusion
  15.8 101.9 %shard_map.77 = f32[8,128,256]{2,1,0:T(8,128)} custom-call(s32[8,128]{1,0:T(8,128)} %bitcast.40, s32[64]{0:T(128)} %get-tuple-element.7.idx, bf16[8,128,256]{2,1,0:T(8,128)(2,1)} %bitcast.38, bf16[32,2,128,128]{3,2,1,0:T(8,128)(2,1)} %bitcast.35), custom_call_target="tpu_custom_call" | custom-call | tf_op jit(solution)/shard_map/pallas_call | solution.py:215
  117.7 2.8 %fusion.7 = (bf16[1024,256]{1,0:T(8,128)(2,1)}, bf16[1024,256]{1,0:T(8,128)(2,1)}) fusion(f32[8,128,256]{2,1,0:T(8,128)} %shard_map.77, bf16[4096,256]{1,0:T(8,128)(2,1)} %param.9, s32[]{:T(128)S(6)} %select_n.68), kind=kLoop, calls=%fused_computation.11 | loop fusion | flops 3145728 | bytes 2621444 | tf_op jit(solution)/shard_map/convert_element_type | solution.py:356
  120.5 96.8 %shard_map.78 = f32[8,128,256]{2,1,0:T(8,128)} custom-call(s32[8,128]{1,0:T(8,128)} %bitcast.41, s32[64]{0:T(128)} %get-tuple-element.7.idx, bf16[8,128,256]{2,1,0:T(8,128)(2,1)} %bitcast.39, bf16[32,2,128,128]{3,2,1,0:T(8,128)(2,1)} %bitcast.36), custom_call_target="tpu_custom_call" | custom-call | tf_op jit(solution)/shard_map/pallas_call | solution.py:215
  217.3 28.8 %shard_map.79 = (bf16[1024,256]{1,0:T(8,128)(2,1)}, f32[256,256]{1,0:T(8,128)}) custom-call(bf16[1024,256]{1,0:T(8,128)(2,1)} %f_ref.1, f32[1024,256]{1,0:T(8,128)} %bitcast.37, bf16[256,256]{1,0:T(8,128)(2,1)} %w_ref.1), custom_call_target="tpu_custom_call" | custom-call | tf_op jit(solution)/shard_map/pallas_call | solution.py:311
  246.1 1.9 copy.17
  248.0 1.7 copy.18
  (1 shorter events, 0.0 us)

commit v2 on v1

v2 whole, which is shorter than its diff:
```python
import functools
import math

import jax
import jax.numpy as jnp
from jax import lax
from jax.experimental import pallas as pl
from jax.experimental.pallas import tpu as pltpu
from jax.sharding import PartitionSpec as P

MESH = pl.DeviceIdType.MESH
Z = 8
YC = 8
X = 4
B = 128
LANES = 128
OWN = 8
F32 = jnp.float32
BF16 = jnp.bfloat16


def place():
    r, c = lax.axis_index("rows"), lax.axis_index("rep")
    return r, r // YC, r % YC, c


def greet(partners):
    barrier = pltpu.get_barrier_semaphore()
    for device in partners:
        pl.semaphore_signal(barrier, inc=1, device_id=device, device_id_type=MESH)
    pl.semaphore_wait(barrier, len(partners))


def remote(src, dst, send, recv, device):
    return pltpu.make_async_remote_copy(
        src_ref=src, dst_ref=dst, send_sem=send, recv_sem=recv, device_id=device, device_id_type=MESH
    )


def wait_bytes(ref, sem):
    pltpu.make_async_copy(ref, ref, sem).wait()


def layer_kernel(
    scale, own_tab, idx, f_ref, w_ref, vals_hbm, grad_hbm, act_ref, ig_ref, wg_ref, *scratch
):
    ag = [scratch[n * Z : (n + 1) * Z] for n in range(4)]
    at = 4 * Z
    sbuf, src, xs, xr, own = (scratch[at + 4 * i : at + 4 * i + 4] for i in range(5))
    at += 20
    (got, tab, vals, grad, ft, high, ig_acc, part, r1, a1, r2, a2, r3, r4, r5) = scratch[at : at + 15]
    at += 15
    (t_send, t_recv, l_sem, z_send, z_recv, y_send, y_recv, x_send, x_recv) = scratch[at : at + 9]
    s1, v1, s2, v2, s3, v3, s4, v4, s5, v5 = scratch[at + 9 :]
    r, z, yc, c = place()
    half = OWN // 2
    peers_x = [(r, (c + d) % X) for d in range(1, X)]
    peers_y = [(z * YC + (yc + 1 + j) % YC, c) for j in range(YC - 1)]
    peers_z = [((z + 1 + i) % Z * YC + yc, c) for i in range(Z - 1)]
    up, down = peers_z[0], peers_z[Z - 2]

    load_vals = pltpu.make_async_copy(vals_hbm, vals, l_sem.at[0])
    load_grad = pltpu.make_async_copy(grad_hbm.at[pl.ds(c * OWN, OWN)], grad, l_sem.at[1])
    load_vals.start()
    load_grad.start()

    def columns(h):
        return pl.ds(h * LANES, LANES)

    def mix(h):
        def row(p, _):
            ag[h][0][p] = jnp.dot(f_ref[p], w_ref[:, columns(h)], preferred_element_type=F32).astype(BF16)
            return 0

        lax.fori_loop(0, OWN, row, 0)

    mix(0)
    greet(peers_x + peers_y + peers_z)

    def hop(n, k, forward):
        nxt = (k + 1) % Z if forward else (k - 1) % Z
        source, target = ag[n][k], ag[n][nxt]
        lane = 0 if forward else 1
        if nxt == Z // 2:
            rows = pl.ds(0, half) if forward else pl.ds(half, half)
            source, target = source.at[rows], target.at[rows]
        return remote(source, target, z_send.at[n, nxt, lane], z_recv.at[n, nxt, lane], up if forward else down)

    def arrived(n, k, lane):
        if k == Z // 2:
            chunk = ag[n][k].at[pl.ds(0 if lane == 0 else half, half)]
        else:
            chunk = ag[n][k]
        wait_bytes(chunk, z_recv.at[n, k, lane])

    def serve(n, k):
        column = (z - k + Z) % Z * YC + yc

        def pick(j, _):
            sbuf[n][j * Z + k] = ag[n][k][tab[YC - 2 - j, column]]
            return 0

        lax.fori_loop(0, YC - 1, pick, 0)
        if k == 0:
            for p in range(OWN):
                src[n][YC * Z + p] = ag[n][0][p]
        else:
            src[n][(YC - 1) * Z + k] = ag[n][k][tab[YC - 1, column]]

        def post(j, _):
            slot = j * Z + k
            target = (z * YC + (yc + 1 + j) % YC, c)
            remote(sbuf[n].at[slot], src[n].at[slot], y_send.at[n], y_recv.at[n], target).start()
            return 0

        lax.fori_loop(0, YC - 1, post, 0)

    def products(n):
        wait_bytes(src[n].at[pl.ds(0, (YC - 1) * Z)], y_recv.at[n])
        for d in (2, 1, 3, 0):
            first = (c + d) % X * OWN

            def post(p):
                slot = (d - 1) * OWN + p
                remote(xs[n].at[slot], xr[n].at[slot], x_send.at[n], x_recv.at[n], (r, (c + d) % X)).start()

            def row(p, _):
                b = first + p
                total = jnp.dot(vals[b, 0], src[n][idx[2 * b]], preferred_element_type=F32)
                total += jnp.dot(vals[b, 1], src[n][idx[2 * b + 1]], preferred_element_type=F32)
                if d == 0:
                    own[n][p] = total
                else:
                    xs[n][(d - 1) * OWN + p] = total.astype(BF16)

                    @pl.when(p > 0)
                    def _():
                        post(p - 1)

                return 0

            lax.fori_loop(0, OWN, row, 0)
            if d != 0:
                post(OWN - 1)

    def summed(n, p):
        a, b, e = (xr[n][d * OWN + p].astype(F32) for d in range(X - 1))
        return (own[n][p] + a) + (b + e)

    def activate(h):
        wait_bytes(xr[h], x_recv.at[h])

        def row(p, _):
            value, slope = silu_parts(summed(h, p))
            act_ref[p, :, columns(h)] = value.astype(BF16)
            ag[2 + h][0][p] = (grad[p, :, columns(h)].astype(F32) * slope).astype(BF16)
            return 0

        lax.fori_loop(0, OWN, row, 0)

    def back(h):
        n = 2 + h
        wait_bytes(xr[n], x_recv.at[n])
        part[h] = jnp.zeros_like(part[h])

        def row(p, _):
            total = summed(n, p)
            top = total.astype(BF16)
            rest = (total - top.astype(F32)).astype(BF16)
            part[h] += jnp.dot(ft[p], top, preferred_element_type=F32) + jnp.dot(
                ft[p], rest, preferred_element_type=F32
            )
            high[h, p] = top
            return 0

        lax.fori_loop(0, OWN, row, 0)

    def input_term(h, p):
        return lax.dot_general(
            high[h, p], w_ref[:, columns(h)], (((1,), (1,)), ((), ())), preferred_element_type=F32
        )

    def ring(n, step):
        if step < Z // 2:
            arrived(n, step, 0)
            hop(n, step, True).start()
            arrived(n, Z - step, 1)
            hop(n, Z - step, False).start()
            serve(n, step)
            serve(n, Z - step)
        else:
            arrived(n, step, 0)
            arrived(n, step, 1)
            serve(n, step)

    def begin(n):
        hop(n, 0, True).start()
        hop(n, 0, False).start()

    begin(0)
    tables = [remote(own_tab, got.at[j], t_send.at[j], t_recv.at[j], peers_y[j]) for j in range(YC - 1)]
    for copy in tables:
        copy.start()
    mix(1)
    for copy in tables:
        copy.wait()
    rows = [got.at[j, 0] for j in range(YC - 1)] + [own_tab.at[0]]
    moves = [pltpu.make_async_copy(row, tab.at[j], l_sem.at[2 + j]) for j, row in enumerate(rows)]
    for move in moves:
        move.start()
    for move in moves:
        move.wait()

    serve(0, 0)
    ring(0, 1)
    begin(1)
    serve(1, 0)
    for p in range(OWN):
        ft[p] = f_ref[p].T
    ring(0, 2)
    ring(0, 3)
    ring(1, 1)
    ring(0, 4)
    load_vals.wait()
    load_grad.wait()
    products(0)
    ring(1, 2)
    ring(1, 3)
    activate(0)
    begin(2)
    serve(2, 0)
    ring(1, 4)
    products(1)
    ring(2, 1)
    ring(2, 2)
    activate(1)
    begin(3)
    serve(3, 0)
    ring(2, 3)
    ring(3, 1)
    ring(2, 4)
    products(2)
    ring(3, 2)
    ring(3, 3)
    back(0)
    ring(3, 4)
    products(3)

    def first_term(p, _):
        ig_acc[p] = input_term(0, p)
        return 0

    lax.fori_loop(0, OWN, first_term, 0)
    back(1)

    share = part.shape[1] // X
    small = share // YC

    def share_of(d):
        return pl.ds(pl.multiple_of((c + d) % X * share, share), share)

    def small_of(j):
        return pl.ds(pl.multiple_of((yc + 1 + j) % YC * small, small), small)

    one = [
        remote(part.at[:, share_of(d)], r1.at[d - 1], s1.at[d - 1], v1.at[d - 1], peers_x[d - 1]) for d in range(1, X)
    ]
    for copy in one:
        copy.start()

    def second_term(p, _):
        ig_ref[p] = (ig_acc[p] + input_term(1, p)).astype(BF16)
        return 0

    lax.fori_loop(0, OWN, second_term, 0)
    for copy in one:
        copy.wait()
    a1[...] = (part[:, share_of(0)] + r1[0]) + (r1[1] + r1[2])
    two = [remote(a1.at[:, small_of(j)], r2.at[j], s2.at[j], v2.at[j], peers_y[j]) for j in range(YC - 1)]
    for copy in two:
        copy.start()
    for copy in two:
        copy.wait()
    total = a1[:, small_of(YC - 1)]
    for j in range(YC - 1):
        total = total + r2[j]
    a2[...] = total
    r3[z] = total
    three = [remote(a2, r3.at[z], s3.at[i], v3.at[i], peers_z[i]) for i in range(Z - 1)]
    for copy in three:
        copy.start()
    for i in range(Z - 1):
        remote(a2, r3.at[(z + Z - 1 - i) % Z], s3.at[i], v3.at[i], peers_z[i]).wait()
    total = r3[0]
    for i in range(1, Z):
        total = total + r3[i]
    r4[yc] = total * scale
    four = [remote(r4.at[yc], r4.at[yc], s4.at[j], v4.at[j], peers_y[j]) for j in range(YC - 1)]
    for copy in four:
        copy.start()
    for j in range(YC - 1):
        remote(r4.at[yc], r4.at[(yc + YC - 1 - j) % YC], s4.at[j], v4.at[j], peers_y[j]).wait()
    five = [remote(r4, r5.at[c], s5.at[d], v5.at[d], peers_x[d]) for d in range(X - 1)]
    for copy in five:
        copy.start()
    r5[c] = r4[...]
    for d in range(X - 1):
        remote(r4, r5.at[(c + X - 1 - d) % X], s5.at[d], v5.at[d], peers_x[d]).wait()
    for q in range(X):
        for j in range(YC):
            for h in range(2):
                wg_ref[pl.ds((q * YC + j) * small, small), columns(h)] = r5[q, j, h]

    for n in range(4):
        for k in range(Z // 2):
            hop(n, k, True).wait_send()
            hop(n, (Z - k) % Z, False).wait_send()
        wait_bytes(sbuf[n], y_send.at[n])
        wait_bytes(xs[n], x_send.at[n])


def layer(own_tab, idx, features, weight, vals, out_grad, node_total):
    width = weight.shape[0]
    share = width // X
    small = share // YC
    blocks = lambda n, kind: pltpu.VMEM((n, B, LANES), kind)
    smem = pl.BlockSpec(memory_space=pltpu.SMEM)
    vmem = pl.BlockSpec(memory_space=pltpu.VMEM)
    hbm = pl.BlockSpec(memory_space=pl.ANY)
    dma = lambda *shape: pltpu.SemaphoreType.DMA(shape)
    wide = jax.ShapeDtypeStruct(features.shape, BF16)
    return pl.pallas_call(
        functools.partial(layer_kernel, 1.0 / math.sqrt(node_total)),
        out_shape=(wide, wide, jax.ShapeDtypeStruct((width, width), F32)),
        in_specs=[vmem, smem, vmem, vmem, hbm, hbm],
        out_specs=(vmem, vmem, vmem),
        scratch_shapes=[blocks(OWN, BF16) for _ in range(4 * Z)]
        + [blocks((YC - 1) * Z, BF16)] * 4
        + [blocks(YC * Z + OWN, BF16)] * 4
        + [blocks((X - 1) * OWN, BF16)] * 8
        + [blocks(OWN, F32)] * 4
        + [
            pltpu.VMEM((YC - 1, 8, LANES), jnp.int32),
            pltpu.SMEM((YC, LANES), jnp.int32),
            pltpu.VMEM(vals.shape, BF16),
            pltpu.VMEM(features.shape, BF16),
            pltpu.VMEM((OWN, width, B), BF16),
            pltpu.VMEM((2, OWN, B, LANES), BF16),
            pltpu.VMEM((OWN, B, width), F32),
            pltpu.VMEM((2, width, LANES), F32),
            pltpu.VMEM((X - 1, 2, share, LANES), F32),
            pltpu.VMEM((2, share, LANES), F32),
            pltpu.VMEM((YC - 1, 2, small, LANES), F32),
            pltpu.VMEM((2, small, LANES), F32),
            pltpu.VMEM((Z, 2, small, LANES), F32),
            pltpu.VMEM((YC, 2, small, LANES), F32),
            pltpu.VMEM((X, YC, 2, small, LANES), F32),
        ]
        + [dma(YC - 1), dma(YC - 1), dma(2 + YC), dma(4, Z, 2), dma(4, Z, 2), dma(4), dma(4), dma(4), dma(4)]
        + [dma(X - 1)] * 2
        + [dma(YC - 1)] * 2
        + [dma(Z - 1)] * 2
        + [dma(YC - 1)] * 2
        + [dma(X - 1)] * 2,
        compiler_params=pltpu.CompilerParams(
            collective_id=0, has_side_effects=True, vmem_limit_bytes=60 * 1024 * 1024
        ),
    )(own_tab, idx, features, weight, vals, out_grad)


def silu_parts(summed):
    sigmoid_vals = jax.nn.sigmoid(summed)
    return (summed * sigmoid_vals, sigmoid_vals * (1.0 + summed * (1.0 - sigmoid_vals)))


def on_device(features, weight, block_cols, block_vals, out_grad):
    own_rows, width = features.shape
    r, z, yc, c = place()
    flat = block_cols[:, 0].reshape(-1)
    owners, places = flat // OWN, flat % OWN
    slot = (yc + YC - 1 - owners % YC) % YC * Z + (z + Z - owners // YC) % Z
    idx = jnp.where(owners == r, YC * Z + places, slot)
    groups = jnp.arange(LANES, dtype=jnp.int32)
    wanted = (owners[:, None] == groups[None, :]) & (owners != r)[:, None]
    table = jnp.sum(jnp.where(wanted, places[:, None], 0), axis=0)
    own_tab = jnp.broadcast_to(table[None], (8, LANES))
    activations, input_grad, weight_grad = layer(
        own_tab,
        idx,
        features.reshape(OWN, B, width),
        weight,
        block_vals[:, 0],
        out_grad.reshape(-1, B, width),
        own_rows * Z * YC * X,
    )
    return (activations.reshape(own_rows, width), input_grad.reshape(own_rows, width), weight_grad)


def solution(mesh):
    placed = (
        P(("rows", "rep"), None),
        P(),
        P("rows", "rep", None),
        P("rows", "rep", None, None, None),
        P("rows", None),
    )
    return jax.shard_map(
        on_device,
        mesh=mesh,
        in_specs=placed,
        out_specs=(P(("rows", "rep"), None), P(("rows", "rep"), None), P()),
        check_vma=False,
    )
```

time: 250 us -> 192 us (0.77)
  Pallas kernels: 237 us -> 184 us
  other arithmetic: 3.44 us -> 0.66 us
    pallas_call x4 -> x1, Pallas kernels: 237 us -> 184 us  [layer(): pl.pallas_call(functools.partial(layer_kernel, 1.0 / math.sqrt(node_total...]
    convert_element_type x1 -> x0, other arithmetic: 2.79 us -> none  [on_device(): masked = (own_grad.astype(F32) * slopes).astype(BF16)]
    unnamed x3 -> x6, local copies, waits for them, and re-layouts: 4.3 us -> 5.25 us
where the time goes in v2:
time: 192 us; the launch traced here: 191 us
  Pallas kernels  184 us (96%)
  local copies, waits for them, and re-layouts  5.95 us (3%)
    pallas_call x1, Pallas kernels, layer(): pl.pallas_call(functools.partial(layer_kernel, 1.0 / math.sqrt(node_total...  184 us
    unnamed x6, local copies, waits for them, and re-layouts  5.25 us

profile of v2, /device:TPU:1, one launch (start us, length us, event | category | flops | bytes accessed | tf_op | source)
XLA Modules:
  0.0 191.4 jit_solution(15581766244240155792)
XLA Ops:
  0.7 0.8 copy.10
  1.4 0.1 reshape_squeeze.3
  1.5 0.5 compare_select_fusion.4
  2.1 0.1 select_reduce_fusion
  2.2 0.6 broadcast_in_dim.24.own_tab
  2.8 184.1 %shard_map.76 = (bf16[8,128,256]{2,1,0:T(8,128)(2,1)}, bf16[8,128,256]{2,1,0:T(8,128)(2,1)}, f32[256,256]{1,0:T(8,128)}) custom-call(s32[8,128]{1,0:T(8,128)} %broadcast_in_dim.24.own_tab, s32[64]{0:T(128)} %get-tuple-element.9.idx, bf16[8,128,256]{2,1,0:T(8,128)(2,1)} %bitcast.9, bf16[256,256]{1,0:T(8,128)(2,1)} %w_ref.1, ...), custom_call_target="tpu_custom_call" | custom-call | tf_op jit(solution)/shard_map/pallas_call | solution.py:332
  186.9 0.0 copy-start
  186.9 1.9 copy.14
  188.8 1.9 copy.15
  190.7 0.0 copy-done
  190.7 0.7 copy.16
  (1 shorter events, 0.0 us)
Async XLA Ops:
  186.9 3.8 %copy-start = (f32[256,256]{1,0:T(8,128)S(1)}, f32[256,256]{1,0:T(8,128)}, u32[]{:S(2)}) copy-start(f32[256,256]{1,0:T(8,128)} %get-tuple-element.17) | copy-start | bytes 786436

commit v3 on v2

--- a/solution.py
+++ b/solution.py
@@ -25,10 +25,8 @@
 
 
 def greet(partners):
-    barrier = pltpu.get_barrier_semaphore()
     for device in partners:
-        pl.semaphore_signal(barrier, inc=1, device_id=device, device_id_type=MESH)
-    pl.semaphore_wait(barrier, len(partners))
+        pl.semaphore_signal(pltpu.get_barrier_semaphore(), inc=1, device_id=device, device_id_type=MESH)
 
 
 def remote(src, dst, send, recv, device):
@@ -42,14 +40,15 @@
 
 
 def layer_kernel(
-    scale, own_tab, idx, f_ref, w_ref, vals_hbm, grad_hbm, act_ref, ig_ref, wg_ref, *scratch
+    scale, own_tab, idx, f_hbm, w_ref, vals_hbm, grad_hbm, act_hbm, ig_hbm, wg_ref, *scratch
 ):
     ag = [scratch[n * Z : (n + 1) * Z] for n in range(4)]
     at = 4 * Z
     sbuf, src, xs, xr, own = (scratch[at + 4 * i : at + 4 * i + 4] for i in range(5))
     at += 20
-    (got, tab, vals, grad, ft, high, ig_acc, part, r1, a1, r2, a2, r3, r4, r5) = scratch[at : at + 15]
-    at += 15
+    (got, tab, f_ref, act_ref, ig_ref, vals, grad, ft, high, ig_acc, part) = scratch[at : at + 11]
+    (r1, a1, r2, a2, r3, r4, r5) = scratch[at + 11 : at + 18]
+    at += 18
     (t_send, t_recv, l_sem, z_send, z_recv, y_send, y_recv, x_send, x_recv) = scratch[at : at + 9]
     s1, v1, s2, v2, s3, v3, s4, v4, s5, v5 = scratch[at + 9 :]
     r, z, yc, c = place()
@@ -59,10 +58,15 @@
     peers_z = [((z + 1 + i) % Z * YC + yc, c) for i in range(Z - 1)]
     up, down = peers_z[0], peers_z[Z - 2]
 
-    load_vals = pltpu.make_async_copy(vals_hbm, vals, l_sem.at[0])
+    load_features = pltpu.make_async_copy(f_hbm, f_ref, l_sem.at[2])
+    load_features.start()
+    greet(peers_x + peers_y + peers_z)
     load_grad = pltpu.make_async_copy(grad_hbm.at[pl.ds(c * OWN, OWN)], grad, l_sem.at[1])
-    load_vals.start()
-    load_grad.start()
+    load_vals = [
+        pltpu.make_async_copy(vals_hbm.at[:, s], vals.at[:, :, pl.ds(s * B, B)], l_sem.at[3 * s]) for s in range(2)
+    ]
+    save_act = pltpu.make_async_copy(act_ref, act_hbm, l_sem.at[4])
+    save_ig = pltpu.make_async_copy(ig_ref, ig_hbm, l_sem.at[5])
 
     def columns(h):
         return pl.ds(h * LANES, LANES)
@@ -74,8 +78,9 @@
 
         lax.fori_loop(0, OWN, row, 0)
 
+    load_features.wait()
     mix(0)
-    greet(peers_x + peers_y + peers_z)
+    pl.semaphore_wait(pltpu.get_barrier_semaphore(), X + YC + Z - 3)
 
     def hop(n, k, forward):
         nxt = (k + 1) % Z if forward else (k - 1) % Z
@@ -115,33 +120,30 @@
 
         lax.fori_loop(0, YC - 1, post, 0)
 
-    def products(n):
+    def products(n, classes):
+        for d in classes:
+            first = (c + d) % X * OWN
+
+            def pair(q, _):
+                totals = []
+                for p in (2 * q, 2 * q + 1):
+                    b = first + p
+                    used = jnp.concatenate([src[n][idx[2 * b]], src[n][idx[2 * b + 1]]], axis=0)
+                    totals.append(jnp.dot(vals[b], used, preferred_element_type=F32))
+                if d == 0:
+                    own[n][2 * q], own[n][2 * q + 1] = totals
+                else:
+                    at = (d - 1) * OWN + 2 * q
+                    xs[n][at], xs[n][at + 1] = [total.astype(BF16) for total in totals]
+                    both = pl.ds(at, 2)
+                    target = (r, (c + d) % X)
+                    remote(xs[n].at[both], xr[n].at[both], x_send.at[n], x_recv.at[n], target).start()
+                return 0
+
+            lax.fori_loop(0, OWN // 2, pair, 0)
+
+    def gathered(n):
         wait_bytes(src[n].at[pl.ds(0, (YC - 1) * Z)], y_recv.at[n])
-        for d in (2, 1, 3, 0):
-            first = (c + d) % X * OWN
-
-            def post(p):
-                slot = (d - 1) * OWN + p
-                remote(xs[n].at[slot], xr[n].at[slot], x_send.at[n], x_recv.at[n], (r, (c + d) % X)).start()
-
-            def row(p, _):
-                b = first + p
-                total = jnp.dot(vals[b, 0], src[n][idx[2 * b]], preferred_element_type=F32)
-                total += jnp.dot(vals[b, 1], src[n][idx[2 * b + 1]], preferred_element_type=F32)
-                if d == 0:
-                    own[n][p] = total
-                else:
-                    xs[n][(d - 1) * OWN + p] = total.astype(BF16)
-
-                    @pl.when(p > 0)
-                    def _():
-                        post(p - 1)
-
-                return 0
-
-            lax.fori_loop(0, OWN, row, 0)
-            if d != 0:
-                post(OWN - 1)
 
     def summed(n, p):
         a, b, e = (xr[n][d * OWN + p].astype(F32) for d in range(X - 1))
@@ -201,56 +203,68 @@
     tables = [remote(own_tab, got.at[j], t_send.at[j], t_recv.at[j], peers_y[j]) for j in range(YC - 1)]
     for copy in tables:
         copy.start()
+    load_grad.start()
+    for load in load_vals:
+        load.start()
     mix(1)
     for copy in tables:
         copy.wait()
     rows = [got.at[j, 0] for j in range(YC - 1)] + [own_tab.at[0]]
-    moves = [pltpu.make_async_copy(row, tab.at[j], l_sem.at[2 + j]) for j, row in enumerate(rows)]
+    moves = [pltpu.make_async_copy(row, tab.at[j], l_sem.at[6 + j]) for j, row in enumerate(rows)]
     for move in moves:
         move.start()
     for move in moves:
         move.wait()
 
     serve(0, 0)
-    ring(0, 1)
-    begin(1)
     serve(1, 0)
     for p in range(OWN):
         ft[p] = f_ref[p].T
+    ring(0, 1)
     ring(0, 2)
     ring(0, 3)
+    begin(1)
+    ring(0, 4)
+    load_grad.wait()
+    for load in load_vals:
+        load.wait()
     ring(1, 1)
-    ring(0, 4)
-    load_vals.wait()
-    load_grad.wait()
-    products(0)
+    gathered(0)
+    products(0, (2, 1))
     ring(1, 2)
+    products(0, (3, 0))
     ring(1, 3)
     activate(0)
     begin(2)
+    ring(1, 4)
     serve(2, 0)
-    ring(1, 4)
-    products(1)
+    gathered(1)
+    products(1, (2, 1))
     ring(2, 1)
+    products(1, (3, 0))
     ring(2, 2)
     activate(1)
-    begin(3)
+    save_act.start()
     serve(3, 0)
     ring(2, 3)
+    begin(3)
+    ring(2, 4)
     ring(3, 1)
-    ring(2, 4)
-    products(2)
+    gathered(2)
+    products(2, (2, 1))
     ring(3, 2)
+    products(2, (3, 0))
     ring(3, 3)
+    ring(3, 4)
     back(0)
-    ring(3, 4)
-    products(3)
 
     def first_term(p, _):
         ig_acc[p] = input_term(0, p)
         return 0
 
     lax.fori_loop(0, OWN, first_term, 0)
+    gathered(3)
+    products(3, (2, 1, 3, 0))
     back(1)
 
     share = part.shape[1] // X
@@ -273,6 +287,7 @@
         return 0
 
     lax.fori_loop(0, OWN, second_term, 0)
+    save_ig.start()
     for copy in one:
         copy.wait()
     a1[...] = (part[:, share_of(0)] + r1[0]) + (r1[1] + r1[2])
@@ -311,6 +326,8 @@
             for h in range(2):
                 wg_ref[pl.ds((q * YC + j) * small, small), columns(h)] = r5[q, j, h]
 
+    save_act.wait()
+    save_ig.wait()
     for n in range(4):
         for k in range(Z // 2):
             hop(n, k, True).wait_send()
@@ -332,8 +349,8 @@
     return pl.pallas_call(
         functools.partial(layer_kernel, 1.0 / math.sqrt(node_total)),
         out_shape=(wide, wide, jax.ShapeDtypeStruct((width, width), F32)),
-        in_specs=[vmem, smem, vmem, vmem, hbm, hbm],
-        out_specs=(vmem, vmem, vmem),
+        in_specs=[vmem, smem, hbm, vmem, hbm, hbm],
+        out_specs=(hbm, hbm, vmem),
         scratch_shapes=[blocks(OWN, BF16) for _ in range(4 * Z)]
         + [blocks((YC - 1) * Z, BF16)] * 4
         + [blocks(YC * Z + OWN, BF16)] * 4
@@ -342,7 +359,10 @@
         + [
             pltpu.VMEM((YC - 1, 8, LANES), jnp.int32),
             pltpu.SMEM((YC, LANES), jnp.int32),
-            pltpu.VMEM(vals.shape, BF16),
+            pltpu.VMEM(features.shape, BF16),
+            pltpu.VMEM(features.shape, BF16),
+            pltpu.VMEM(features.shape, BF16),
+            pltpu.VMEM((vals.shape[0], B, 2 * B), BF16),
             pltpu.VMEM(features.shape, BF16),
             pltpu.VMEM((OWN, width, B), BF16),
             pltpu.VMEM((2, OWN, B, LANES), BF16),
@@ -356,7 +376,7 @@
             pltpu.VMEM((YC, 2, small, LANES), F32),
             pltpu.VMEM((X, YC, 2, small, LANES), F32),
         ]
-        + [dma(YC - 1), dma(YC - 1), dma(2 + YC), dma(4, Z, 2), dma(4, Z, 2), dma(4), dma(4), dma(4), dma(4)]
+        + [dma(YC - 1), dma(YC - 1), dma(6 + YC), dma(4, Z, 2), dma(4, Z, 2), dma(4), dma(4), dma(4), dma(4)]
         + [dma(X - 1)] * 2
         + [dma(YC - 1)] * 2
         + [dma(Z - 1)] * 2

time: 192 us -> 164 us (0.85)
  Pallas kernels: 184 us -> 156 us
    pallas_call x1, Pallas kernels: 184 us -> 156 us  [layer(): pl.pallas_call(functools.partial(layer_kernel, 1.0 / math.sqrt(node_total...]
where the time goes in v3:
time: 164 us; the launch traced here: 163 us
  Pallas kernels  156 us (95%)
  local copies, waits for them, and re-layouts  5.95 us (4%)
    pallas_call x1, Pallas kernels, layer(): pl.pallas_call(functools.partial(layer_kernel, 1.0 / math.sqrt(node_total...  156 us
    unnamed x6, local copies, waits for them, and re-layouts  5.25 us

profile of v3, /device:TPU:1, one launch (start us, length us, event | category | flops | bytes accessed | tf_op | source)
XLA Modules:
  0.0 163.4 jit_solution(14787857947694682891)
XLA Ops:
  0.7 0.8 copy.10
  1.4 0.1 reshape_squeeze.3
  1.5 0.5 compare_select_fusion.4
  2.1 0.1 select_reduce_fusion
  2.2 0.6 broadcast_in_dim.24.own_tab
  2.8 156.1 %shard_map.76 = (bf16[8,128,256]{2,1,0:T(8,128)(2,1)}, bf16[8,128,256]{2,1,0:T(8,128)(2,1)}, f32[256,256]{1,0:T(8,128)}) custom-call(s32[8,128]{1,0:T(8,128)} %broadcast_in_dim.24.own_tab, s32[64]{0:T(128)} %get-tuple-element.9.idx, bf16[8,128,256]{2,1,0:T(8,128)(2,1)} %bitcast.9, bf16[256,256]{1,0:T(8,128)(2,1)} %w_ref.1, ...), custom_call_target="tpu_custom_call" | custom-call | tf_op jit(solution)/shard_map/pallas_call | solution.py:349
  158.9 0.0 copy-start
  158.9 1.9 %copy.14 = bf16[1024,256]{1,0:T(8,128)(2,1)} copy(bf16[1024,256]{1,0:T(8,128)(2,1)} %bitcast.11) | data formatting | bytes 1048576
  160.8 1.9 %copy.15 = bf16[1024,256]{1,0:T(8,128)(2,1)} copy(bf16[1024,256]{1,0:T(8,128)(2,1)} %bitcast.10) | data formatting | bytes 1048576
  162.7 0.0 copy-done
  162.7 0.7 copy.16
  (1 shorter events, 0.0 us)
Async XLA Ops:
  158.9 3.8 %copy-start = (f32[256,256]{1,0:T(8,128)S(1)}, f32[256,256]{1,0:T(8,128)}, u32[]{:S(2)}) copy-start(f32[256,256]{1,0:T(8,128)} %get-tuple-element.17) | copy-start | bytes 786436

commit v4 on v3

--- a/solution.py
+++ b/solution.py
@@ -15,6 +15,7 @@
 B = 128
 LANES = 128
 OWN = 8
+PLANE = X * YC
 F32 = jnp.float32
 BF16 = jnp.bfloat16
 
@@ -24,9 +25,8 @@
     return r, r // YC, r % YC, c
 
 
-def greet(partners):
-    for device in partners:
-        pl.semaphore_signal(pltpu.get_barrier_semaphore(), inc=1, device_id=device, device_id_type=MESH)
+def greet(device):
+    pl.semaphore_signal(pltpu.get_barrier_semaphore(), inc=1, device_id=device, device_id_type=MESH)
 
 
 def remote(src, dst, send, recv, device):
@@ -46,21 +46,32 @@
     at = 4 * Z
     sbuf, src, xs, xr, own = (scratch[at + 4 * i : at + 4 * i + 4] for i in range(5))
     at += 20
-    (got, tab, f_ref, act_ref, ig_ref, vals, grad, ft, high, ig_acc, part) = scratch[at : at + 11]
-    (r1, a1, r2, a2, r3, r4, r5) = scratch[at + 11 : at + 18]
-    at += 18
+    (got, tab, f_ref, act_ref, ig_ref, vals, grad, ft, high, parts, part, r1, a2, r3, r4) = scratch[at : at + 15]
+    at += 15
     (t_send, t_recv, l_sem, z_send, z_recv, y_send, y_recv, x_send, x_recv) = scratch[at : at + 9]
-    s1, v1, s2, v2, s3, v3, s4, v4, s5, v5 = scratch[at + 9 :]
+    s1, v1, s2, v2, s3, v3 = scratch[at + 9 :]
     r, z, yc, c = place()
     half = OWN // 2
-    peers_x = [(r, (c + d) % X) for d in range(1, X)]
+    rank = c * YC + yc
+    small = part.shape[1] // PLANE
     peers_y = [(z * YC + (yc + 1 + j) % YC, c) for j in range(YC - 1)]
     peers_z = [((z + 1 + i) % Z * YC + yc, c) for i in range(Z - 1)]
     up, down = peers_z[0], peers_z[Z - 2]
 
     load_features = pltpu.make_async_copy(f_hbm, f_ref, l_sem.at[2])
     load_features.start()
-    greet(peers_x + peers_y + peers_z)
+
+    def in_plane(j):
+        t = (rank + j) % PLANE
+        return (z * YC + t % YC, t // YC), t
+
+    def greet_plane(j, _):
+        greet(in_plane(j)[0])
+        return 0
+
+    for device in peers_z:
+        greet(device)
+    lax.fori_loop(1, PLANE, greet_plane, 0)
     load_grad = pltpu.make_async_copy(grad_hbm.at[pl.ds(c * OWN, OWN)], grad, l_sem.at[1])
     load_vals = [
         pltpu.make_async_copy(vals_hbm.at[:, s], vals.at[:, :, pl.ds(s * B, B)], l_sem.at[3 * s]) for s in range(2)
@@ -72,15 +83,12 @@
         return pl.ds(h * LANES, LANES)
 
     def mix(h):
-        def row(p, _):
-            ag[h][0][p] = jnp.dot(f_ref[p], w_ref[:, columns(h)], preferred_element_type=F32).astype(BF16)
-            return 0
-
-        lax.fori_loop(0, OWN, row, 0)
+        mixed = jnp.dot(f_ref[...].reshape(-1, f_ref.shape[2]), w_ref[:, columns(h)], preferred_element_type=F32)
+        ag[h][0][...] = mixed.astype(BF16).reshape(OWN, B, LANES)
 
     load_features.wait()
     mix(0)
-    pl.semaphore_wait(pltpu.get_barrier_semaphore(), X + YC + Z - 3)
+    pl.semaphore_wait(pltpu.get_barrier_semaphore(), PLANE + Z - 2)
 
     def hop(n, k, forward):
         nxt = (k + 1) % Z if forward else (k - 1) % Z
@@ -163,24 +171,58 @@
     def back(h):
         n = 2 + h
         wait_bytes(xr[n], x_recv.at[n])
-        part[h] = jnp.zeros_like(part[h])
 
         def row(p, _):
+            nodes = pl.ds(pl.multiple_of(p * B, B), B)
             total = summed(n, p)
             top = total.astype(BF16)
-            rest = (total - top.astype(F32)).astype(BF16)
-            part[h] += jnp.dot(ft[p], top, preferred_element_type=F32) + jnp.dot(
-                ft[p], rest, preferred_element_type=F32
-            )
-            high[h, p] = top
+            high[nodes, columns(h)] = top
+            parts[nodes, columns(0)] = top
+            parts[nodes, columns(1)] = (total - top.astype(F32)).astype(BF16)
             return 0
 
         lax.fori_loop(0, OWN, row, 0)
-
-    def input_term(h, p):
-        return lax.dot_general(
-            high[h, p], w_ref[:, columns(h)], (((1,), (1,)), ((), ())), preferred_element_type=F32
-        )
+        both = jnp.dot(ft[...], parts[...], preferred_element_type=F32)
+        part[h] = both[:, :LANES] + both[:, LANES:]
+
+    def share_of(h, t):
+        return part.at[h, pl.ds(pl.multiple_of(t * small, small), small)]
+
+    def spread(h):
+        def post(j, _):
+            target, t = in_plane(j)
+            remote(share_of(h, t), r1.at[h, j - 1], s1.at[h], v1.at[h], target).start()
+            return 0
+
+        lax.fori_loop(1, PLANE, post, 0)
+
+    def collect(h):
+        wait_bytes(r1.at[h], v1.at[h])
+        total = share_of(h, rank)[...]
+        for j in range(PLANE - 1):
+            total = total + r1[h, j]
+        a2[h] = total
+        r3[h, z] = total
+        for i in range(Z - 1):
+            remote(a2.at[h], r3.at[h, z], s2.at[h, i], v2.at[h, i], peers_z[i]).start()
+
+    def share(h):
+        for i in range(Z - 1):
+            remote(a2.at[h], r3.at[h, (z + Z - 1 - i) % Z], s2.at[h, i], v2.at[h, i], peers_z[i]).wait()
+        total = r3[h, 0]
+        for i in range(1, Z):
+            total = total + r3[h, i]
+        r4[h, rank] = total * scale
+
+        def post(j, _):
+            remote(r4.at[h, rank], r4.at[h, rank], s3.at[h], v3.at[h], in_plane(j)[0]).start()
+            return 0
+
+        lax.fori_loop(1, PLANE, post, 0)
+
+    def finish(h):
+        wait_bytes(r4.at[h, pl.ds(0, PLANE - 1)], v3.at[h])
+        wg_ref[:, columns(h)] = r4[h].reshape(-1, LANES)
 
     def ring(n, step):
         if step < Z // 2:
@@ -219,7 +261,7 @@
     serve(0, 0)
     serve(1, 0)
     for p in range(OWN):
-        ft[p] = f_ref[p].T
+        ft[:, p * B : (p + 1) * B] = f_ref[p].T
     ring(0, 1)
     ring(0, 2)
     ring(0, 3)
@@ -258,76 +300,27 @@
     ring(3, 4)
     back(0)
 
-    def first_term(p, _):
-        ig_acc[p] = input_term(0, p)
-        return 0
-
-    lax.fori_loop(0, OWN, first_term, 0)
+    spread(0)
     gathered(3)
-    products(3, (2, 1, 3, 0))
+    products(3, (2, 1))
+    collect(0)
+    products(3, (3, 0))
+    share(0)
     back(1)
-
-    share = part.shape[1] // X
-    small = share // YC
-
-    def share_of(d):
-        return pl.ds(pl.multiple_of((c + d) % X * share, share), share)
-
-    def small_of(j):
-        return pl.ds(pl.multiple_of((yc + 1 + j) % YC * small, small), small)
-
-    one = [
-        remote(part.at[:, share_of(d)], r1.at[d - 1], s1.at[d - 1], v1.at[d - 1], peers_x[d - 1]) for d in range(1, X)
-    ]
-    for copy in one:
-        copy.start()
-
-    def second_term(p, _):
-        ig_ref[p] = (ig_acc[p] + input_term(1, p)).astype(BF16)
-        return 0
-
-    lax.fori_loop(0, OWN, second_term, 0)
+    spread(1)
+    grads = lax.dot_general(high[...], w_ref[...], (((1,), (1,)), ((), ())), preferred_element_type=F32)
+    ig_ref[...] = grads.astype(BF16).reshape(ig_ref.shape)
     save_ig.start()
-    for copy in one:
-        copy.wait()
-    a1[...] = (part[:, share_of(0)] + r1[0]) + (r1[1] + r1[2])
-    two = [remote(a1.at[:, small_of(j)], r2.at[j], s2.at[j], v2.at[j], peers_y[j]) for j in range(YC - 1)]
-    for copy in two:
-        copy.start()
-    for copy in two:
-        copy.wait()
-    total = a1[:, small_of(YC - 1)]
-    for j in range(YC - 1):
-        total = total + r2[j]
-    a2[...] = total
-    r3[z] = total
-    three = [remote(a2, r3.at[z], s3.at[i], v3.at[i], peers_z[i]) for i in range(Z - 1)]
-    for copy in three:
-        copy.start()
-    for i in range(Z - 1):
-        remote(a2, r3.at[(z + Z - 1 - i) % Z], s3.at[i], v3.at[i], peers_z[i]).wait()
-    total = r3[0]
-    for i in range(1, Z):
-        total = total + r3[i]
-    r4[yc] = total * scale
-    four = [remote(r4.at[yc], r4.at[yc], s4.at[j], v4.at[j], peers_y[j]) for j in range(YC - 1)]
-    for copy in four:
-        copy.start()
-    for j in range(YC - 1):
-        remote(r4.at[yc], r4.at[(yc + YC - 1 - j) % YC], s4.at[j], v4.at[j], peers_y[j]).wait()
-    five = [remote(r4, r5.at[c], s5.at[d], v5.at[d], peers_x[d]) for d in range(X - 1)]
-    for copy in five:
-        copy.start()
-    r5[c] = r4[...]
-    for d in range(X - 1):
-        remote(r4, r5.at[(c + X - 1 - d) % X], s5.at[d], v5.at[d], peers_x[d]).wait()
-    for q in range(X):
-        for j in range(YC):
-            for h in range(2):
-                wg_ref[pl.ds((q * YC + j) * small, small), columns(h)] = r5[q, j, h]
+    finish(0)
+    collect(1)
+    share(1)
+    finish(1)
 
     save_act.wait()
     save_ig.wait()
+    for h in range(2):
+        wait_bytes(r1.at[h], s1.at[h])
+        wait_bytes(r4.at[h, pl.ds(0, PLANE - 1)], s3.at[h])
     for n in range(4):
         for k in range(Z // 2):
             hop(n, k, True).wait_send()
@@ -338,8 +331,7 @@
 
 def layer(own_tab, idx, features, weight, vals, out_grad, node_total):
     width = weight.shape[0]
-    share = width // X
-    small = share // YC
+    small = width // PLANE
     blocks = lambda n, kind: pltpu.VMEM((n, B, LANES), kind)
     smem = pl.BlockSpec(memory_space=pltpu.SMEM)
     vmem = pl.BlockSpec(memory_space=pltpu.VMEM)
@@ -364,24 +356,19 @@
             pltpu.VMEM(features.shape, BF16),
             pltpu.VMEM((vals.shape[0], B, 2 * B), BF16),
             pltpu.VMEM(features.shape, BF16),
-            pltpu.VMEM((OWN, width, B), BF16),
-            pltpu.VMEM((2, OWN, B, LANES), BF16),
-            pltpu.VMEM((OWN, B, width), F32),
+            pltpu.VMEM((width, OWN * B), BF16),
+            pltpu.VMEM((OWN * B, width), BF16),
+            pltpu.VMEM((OWN * B, 2 * LANES), BF16),
             pltpu.VMEM((2, width, LANES), F32),
-            pltpu.VMEM((X - 1, 2, share, LANES), F32),
-            pltpu.VMEM((2, share, LANES), F32),
-            pltpu.VMEM((YC - 1, 2, small, LANES), F32),
+            pltpu.VMEM((2, PLANE - 1, small, LANES), F32),
             pltpu.VMEM((2, small, LANES), F32),
-            pltpu.VMEM((Z, 2, small, LANES), F32),
-            pltpu.VMEM((YC, 2, small, LANES), F32),
-            pltpu.VMEM((X, YC, 2, small, LANES), F32),
+            pltpu.VMEM((2, Z, small, LANES), F32),
+            pltpu.VMEM((2, PLANE, small, LANES), F32),
         ]
         + [dma(YC - 1), dma(YC - 1), dma(6 + YC), dma(4, Z, 2), dma(4, Z, 2), dma(4), dma(4), dma(4), dma(4)]
-        + [dma(X - 1)] * 2
-        + [dma(YC - 1)] * 2
-        + [dma(Z - 1)] * 2
-        + [dma(YC - 1)] * 2
-        + [dma(X - 1)] * 2,
+        + [dma(2)] * 2
+        + [dma(2, Z - 1)] * 2
+        + [dma(2)] * 2,
         compiler_params=pltpu.CompilerParams(
             collective_id=0, has_side_effects=True, vmem_limit_bytes=60 * 1024 * 1024
         ),

time: 164 us -> 158 us (0.963)
  Pallas kernels: 156 us -> 150 us
    pallas_call x1, Pallas kernels: 156 us -> 150 us  [layer(): pl.pallas_call(functools.partial(layer_kernel, 1.0 / math.sqrt(node_total...]
where the time goes in v4:
time: 158 us
  Pallas kernels  150 us (95%)
  local copies, waits for them, and re-layouts  5.95 us (4%)
    pallas_call x1, Pallas kernels, layer(): pl.pallas_call(functools.partial(layer_kernel, 1.0 / math.sqrt(node_total...  150 us
    unnamed x6, local copies, waits for them, and re-layouts  5.25 us

profile of v4, /device:TPU:1, one launch (start us, length us, event | category | flops | bytes accessed | tf_op | source)
XLA Modules:
  0.0 157.5 jit_solution(12436226183470716118)
XLA Ops:
  0.7 0.8 copy.10
  1.4 0.1 reshape_squeeze.3
  1.5 0.5 compare_select_fusion.4
  2.1 0.1 select_reduce_fusion
  2.2 0.6 broadcast_in_dim.24.own_tab
  2.8 150.2 %shard_map.76 = (bf16[8,128,256]{2,1,0:T(8,128)(2,1)}, bf16[8,128,256]{2,1,0:T(8,128)(2,1)}, f32[256,256]{1,0:T(8,128)}) custom-call(s32[8,128]{1,0:T(8,128)} %broadcast_in_dim.24.own_tab, s32[64]{0:T(128)} %get-tuple-element.9.idx, bf16[8,128,256]{2,1,0:T(8,128)(2,1)} %bitcast.9, bf16[256,256]{1,0:T(8,128)(2,1)} %w_ref.1, ...), custom_call_target="tpu_custom_call" | custom-call | tf_op jit(solution)/shard_map/pallas_call | solution.py:341
  153.0 0.0 copy-start
  153.0 1.9 %copy.14 = bf16[1024,256]{1,0:T(8,128)(2,1)} copy(bf16[1024,256]{1,0:T(8,128)(2,1)} %bitcast.11) | data formatting | bytes 1048576
  154.9 1.9 %copy.15 = bf16[1024,256]{1,0:T(8,128)(2,1)} copy(bf16[1024,256]{1,0:T(8,128)(2,1)} %bitcast.10) | data formatting | bytes 1048576
  156.8 0.0 copy-done
  156.8 0.7 copy.16
  (1 shorter events, 0.0 us)
Async XLA Ops:
  153.0 3.8 %copy-start = (f32[256,256]{1,0:T(8,128)S(1)}, f32[256,256]{1,0:T(8,128)}, u32[]{:S(2)}) copy-start(f32[256,256]{1,0:T(8,128)} %get-tuple-element.17) | copy-start | bytes 786436

commit v5 on v4

--- a/solution.py
+++ b/solution.py
@@ -46,10 +46,10 @@
     at = 4 * Z
     sbuf, src, xs, xr, own = (scratch[at + 4 * i : at + 4 * i + 4] for i in range(5))
     at += 20
-    (got, tab, f_ref, act_ref, ig_ref, vals, grad, ft, high, parts, part, r1, a2, r3, r4) = scratch[at : at + 15]
+    (got, tab, f_ref, act_ref, ig_ref, vals, grad, ft, high, fx, part, r1, a2, r3, r4) = scratch[at : at + 15]
     at += 15
     (t_send, t_recv, l_sem, z_send, z_recv, y_send, y_recv, x_send, x_recv) = scratch[at : at + 9]
-    s1, v1, s2, v2, s3, v3 = scratch[at + 9 :]
+    s1, v1, s2, v2, s3, v3, f_send, f_recv = scratch[at + 9 :]
     r, z, yc, c = place()
     half = OWN // 2
     rank = c * YC + yc
@@ -174,16 +174,23 @@
 
         def row(p, _):
             nodes = pl.ds(pl.multiple_of(p * B, B), B)
-            total = summed(n, p)
-            top = total.astype(BF16)
-            high[nodes, columns(h)] = top
-            parts[nodes, columns(0)] = top
-            parts[nodes, columns(1)] = (total - top.astype(F32)).astype(BF16)
+            high[nodes, columns(h)] = summed(n, p).astype(BF16)
             return 0
 
         lax.fori_loop(0, OWN, row, 0)
-        both = jnp.dot(ft[...], parts[...], preferred_element_type=F32)
-        part[h] = both[:, :LANES] + both[:, LANES:]
+
+    def flip(d):
+        source = f_ref if d == 0 else fx.at[d - 1]
+        for p in range(OWN):
+            ft[d, :, p * B : (p + 1) * B] = source[p].T
+
+    def terms(h):
+        n = 2 + h
+        total = jnp.dot(ft[0], own[n][...].astype(BF16).reshape(-1, LANES), preferred_element_type=F32)
+        for d in range(1, X):
+            sums = xs[n][(d - 1) * OWN : d * OWN].reshape(-1, LANES)
+            total += jnp.dot(ft[d], sums, preferred_element_type=F32)
+        part[h] = total
 
     def share_of(h, t):
         return part.at[h, pl.ds(pl.multiple_of(t * small, small), small)]
@@ -244,6 +251,11 @@
     begin(0)
     tables = [remote(own_tab, got.at[j], t_send.at[j], t_recv.at[j], peers_y[j]) for j in range(YC - 1)]
     for copy in tables:
+        copy.start()
+    fetch = [
+        remote(f_ref, fx.at[d - 1], f_send.at[d - 1], f_recv.at[d - 1], (r, (c + X - d) % X)) for d in range(1, X)
+    ]
+    for copy in fetch:
         copy.start()
     load_grad.start()
     for load in load_vals:
@@ -260,8 +272,7 @@
 
     serve(0, 0)
     serve(1, 0)
-    for p in range(OWN):
-        ft[:, p * B : (p + 1) * B] = f_ref[p].T
+    flip(0)
     ring(0, 1)
     ring(0, 2)
     ring(0, 3)
@@ -280,6 +291,9 @@
     begin(2)
     ring(1, 4)
     serve(2, 0)
+    for copy in fetch:
+        copy.wait()
+    flip(1)
     gathered(1)
     products(1, (2, 1))
     ring(2, 1)
@@ -290,7 +304,9 @@
     serve(3, 0)
     ring(2, 3)
     begin(3)
+    flip(2)
     ring(2, 4)
+    flip(3)
     ring(3, 1)
     gathered(2)
     products(2, (2, 1))
@@ -298,22 +314,22 @@
     products(2, (3, 0))
     ring(3, 3)
     ring(3, 4)
+    terms(0)
+    spread(0)
     back(0)
-
-    spread(0)
     gathered(3)
-    products(3, (2, 1))
+    products(3, (2, 1, 3, 0))
+    terms(1)
+    spread(1)
     collect(0)
-    products(3, (3, 0))
+    collect(1)
     share(0)
+    share(1)
     back(1)
-    spread(1)
     grads = lax.dot_general(high[...], w_ref[...], (((1,), (1,)), ((), ())), preferred_element_type=F32)
     ig_ref[...] = grads.astype(BF16).reshape(ig_ref.shape)
     save_ig.start()
     finish(0)
-    collect(1)
-    share(1)
     finish(1)
 
     save_act.wait()
@@ -356,9 +372,9 @@
             pltpu.VMEM(features.shape, BF16),
             pltpu.VMEM((vals.shape[0], B, 2 * B), BF16),
             pltpu.VMEM(features.shape, BF16),
-            pltpu.VMEM((width, OWN * B), BF16),
+            pltpu.VMEM((X, width, OWN * B), BF16),
             pltpu.VMEM((OWN * B, width), BF16),
-            pltpu.VMEM((OWN * B, 2 * LANES), BF16),
+            pltpu.VMEM((X - 1, *features.shape), BF16),
             pltpu.VMEM((2, width, LANES), F32),
             pltpu.VMEM((2, PLANE - 1, small, LANES), F32),
             pltpu.VMEM((2, small, LANES), F32),
@@ -368,7 +384,8 @@
         + [dma(YC - 1), dma(YC - 1), dma(6 + YC), dma(4, Z, 2), dma(4, Z, 2), dma(4), dma(4), dma(4), dma(4)]
         + [dma(2)] * 2
         + [dma(2, Z - 1)] * 2
-        + [dma(2)] * 2,
+        + [dma(2)] * 2
+        + [dma(X - 1)] * 2,
         compiler_params=pltpu.CompilerParams(
             collective_id=0, has_side_effects=True, vmem_limit_bytes=60 * 1024 * 1024
         ),

time: 158 us -> 154 us (0.975)
  Pallas kernels: 150 us -> 146 us
    pallas_call x1, Pallas kernels: 150 us -> 146 us  [layer(): pl.pallas_call(functools.partial(layer_kernel, 1.0 / math.sqrt(node_total...]
where the time goes in v5:
time: 154 us; the launch traced here: 153 us
  Pallas kernels  146 us (95%)
  local copies, waits for them, and re-layouts  5.95 us (4%)
    pallas_call x1, Pallas kernels, layer(): pl.pallas_call(functools.partial(layer_kernel, 1.0 / math.sqrt(node_total...  146 us
    unnamed x6, local copies, waits for them, and re-layouts  5.25 us

profile of v5, /device:TPU:1, one launch (start us, length us, event | category | flops | bytes accessed | tf_op | source)
XLA Modules:
  0.0 153.4 jit_solution(15535967181668246572)
XLA Ops:
  0.7 0.8 copy.10
  1.4 0.1 reshape_squeeze.3
  1.5 0.5 compare_select_fusion.4
  2.1 0.1 select_reduce_fusion
  2.2 0.6 broadcast_in_dim.24.own_tab
  2.8 146.2 %shard_map.76 = (bf16[8,128,256]{2,1,0:T(8,128)(2,1)}, bf16[8,128,256]{2,1,0:T(8,128)(2,1)}, f32[256,256]{1,0:T(8,128)}) custom-call(s32[8,128]{1,0:T(8,128)} %broadcast_in_dim.24.own_tab, s32[64]{0:T(128)} %get-tuple-element.9.idx, bf16[8,128,256]{2,1,0:T(8,128)(2,1)} %bitcast.9, bf16[256,256]{1,0:T(8,128)(2,1)} %w_ref.1, ...), custom_call_target="tpu_custom_call" | custom-call | tf_op jit(solution)/shard_map/pallas_call | solution.py:357
  148.9 0.0 copy-start
  149.0 1.9 %copy.14 = bf16[1024,256]{1,0:T(8,128)(2,1)} copy(bf16[1024,256]{1,0:T(8,128)(2,1)} %bitcast.11) | data formatting | bytes 1048576
  150.9 1.9 %copy.15 = bf16[1024,256]{1,0:T(8,128)(2,1)} copy(bf16[1024,256]{1,0:T(8,128)(2,1)} %bitcast.10) | data formatting | bytes 1048576
  152.7 0.0 copy-done
  152.7 0.7 copy.16
  (1 shorter events, 0.0 us)
Async XLA Ops:
  148.9 3.8 %copy-start = (f32[256,256]{1,0:T(8,128)S(1)}, f32[256,256]{1,0:T(8,128)}, u32[]{:S(2)}) copy-start(f32[256,256]{1,0:T(8,128)} %get-tuple-element.17) | copy-start | bytes 786436

commit v6 on v5

--- a/solution.py
+++ b/solution.py
@@ -317,13 +317,13 @@
     terms(0)
     spread(0)
     back(0)
+    collect(0)
     gathered(3)
     products(3, (2, 1, 3, 0))
     terms(1)
     spread(1)
-    collect(0)
+    share(0)
     collect(1)
-    share(0)
     share(1)
     back(1)
     grads = lax.dot_general(high[...], w_ref[...], (((1,), (1,)), ((), ())), preferred_element_type=F32)

time: 154 us -> 155 us (level)
  Pallas kernels: 146 us -> 148 us
    pallas_call x1, Pallas kernels: 146 us -> 148 us  [layer(): pl.pallas_call(functools.partial(layer_kernel, 1.0 / math.sqrt(node_total...]
where the time goes in v6:
time: 155 us
  Pallas kernels  148 us (95%)
  local copies, waits for them, and re-layouts  5.95 us (4%)
    pallas_call x1, Pallas kernels, layer(): pl.pallas_call(functools.partial(layer_kernel, 1.0 / math.sqrt(node_total...  148 us
    unnamed x6, local copies, waits for them, and re-layouts  5.25 us

profile of v6, /device:TPU:1, one launch (start us, length us, event | category | flops | bytes accessed | tf_op | source)
XLA Modules:
  0.0 155.2 jit_solution(13652108445531961359)
XLA Ops:
  0.7 0.8 copy.10
  1.4 0.1 reshape_squeeze.3
  1.5 0.5 compare_select_fusion.4
  2.1 0.1 select_reduce_fusion
  2.2 0.6 broadcast_in_dim.24.own_tab
  2.8 148.0 %shard_map.76 = (bf16[8,128,256]{2,1,0:T(8,128)(2,1)}, bf16[8,128,256]{2,1,0:T(8,128)(2,1)}, f32[256,256]{1,0:T(8,128)}) custom-call(s32[8,128]{1,0:T(8,128)} %broadcast_in_dim.24.own_tab, s32[64]{0:T(128)} %get-tuple-element.9.idx, bf16[8,128,256]{2,1,0:T(8,128)(2,1)} %bitcast.9, bf16[256,256]{1,0:T(8,128)(2,1)} %w_ref.1, ...), custom_call_target="tpu_custom_call" | custom-call | tf_op jit(solution)/shard_map/pallas_call | solution.py:357
  150.7 0.0 copy-start
  150.8 1.9 %copy.14 = bf16[1024,256]{1,0:T(8,128)(2,1)} copy(bf16[1024,256]{1,0:T(8,128)(2,1)} %bitcast.11) | data formatting | bytes 1048576
  152.7 1.9 %copy.15 = bf16[1024,256]{1,0:T(8,128)(2,1)} copy(bf16[1024,256]{1,0:T(8,128)(2,1)} %bitcast.10) | data formatting | bytes 1048576
  154.5 0.0 copy-done
  154.5 0.7 copy.16
  (1 shorter events, 0.0 us)
Async XLA Ops:
  150.7 3.8 %copy-start = (f32[256,256]{1,0:T(8,128)S(1)}, f32[256,256]{1,0:T(8,128)}, u32[]{:S(2)}) copy-start(f32[256,256]{1,0:T(8,128)} %get-tuple-element.17) | copy-start | bytes 786436
